TPU v7x, 256 devices: a whole 4x4x8 slice. The times are simulated.
256 devices in a mesh: col: 32 (over x, y, core), sub: 8 (over z).
Axes of the slice: x: 4, y: 4, z: 8, core: 2. Of those that a mesh axis runs over, the one named last changes fastest.
Arguments:
- vectors: bfloat16 [1048576, 128], P(('col', 'sub')), may hold values from -6 to 6
- near_blocks: bfloat16 [4096, 4, 256, 256], P(('col', 'sub')), may hold values from -0.1875 to 0.1875
- near_index: int32 [4096, 4], P(('col', 'sub')), may hold values from 0 to 4095, as said below
- leaf_basis: bfloat16 [4096, 32, 256], P(('col', 'sub')), may hold values from -0.375 to 0.375
- leaf_transfer: float32 [4096, 32, 32], P(('col', 'sub')), may hold values from -0.25 to 0.25
- leaf_coupling: float32 [4096, 8, 32, 32], P(('col', 'sub')), may hold values from -0.375 to 0.375
- leaf_far: int32 [4096, 8], P(('col', 'sub')), may hold values from 0 to 4095, as said below
- cluster_transfer: float32 [256, 32, 32], P(('col', 'sub')), may hold values from -0.375 to 0.375
- cluster_coupling: float32 [256, 4, 32, 32], P(('col', 'sub')), may hold values from -0.5 to 0.5
- cluster_partner: int32 [256, 4], P(('col', 'sub')), may hold values from 0 to 7
- top_coupling: float32 [32, 8, 32, 32], P('col'), may hold values from -0.375 to 0.375
- top_partner: int32 [32, 8], P('col'), may hold values from 0 to 31
Outputs:
- products: bfloat16 [1048576, 128], P(('col', 'sub'))
Inputs may be any that keep to these rules, and one draw needn't show every extreme that they name: `near_index`: slot 0 of leaf i is i itself; every entry lies within 16 leaves of i; slot 1 is exactly 16 leaves away from i. `leaf_far`: every entry lies within 16 leaves of its row leaf i; slots 0 and 1 are exactly 16 leaves away from i.
All inputs are finite; a program needn't handle non-finite values.
Results may differ from a plain program's by a relative error of at most 0.0034.
Values may be sent and summed in bfloat16 or wider, within the bound.
A program may use at most 64 MiB of HBM per device.

v0:
```python
import jax
import jax.numpy as jnp
from jax import lax
from jax.sharding import PartitionSpec as P

HIGHEST = lax.Precision.HIGHEST


def with_halo(block, sides, width):
    for axis, dim in sides:
        count = lax.axis_size(axis)
        forward = [(i, i + 1) for i in range(count - 1)]
        backward = [(target, source) for source, target in forward]
        low = lax.ppermute(
            lax.slice_in_dim(block, block.shape[dim] - width, None, axis=dim), axis, forward
        )
        high = lax.ppermute(lax.slice_in_dim(block, 0, width, axis=dim), axis, backward)
        block = jnp.concatenate([low, block, high], axis=dim)
    return block


def local(
    vectors,
    near_blocks,
    near_index,
    leaf_basis,
    leaf_transfer,
    leaf_coupling,
    leaf_far,
    cluster_transfer,
    cluster_coupling,
    cluster_partner,
    top_coupling,
    top_partner,
):
    leaves_here = leaf_basis.shape[0]
    leaf_rows = leaf_basis.shape[2]
    columns = vectors.shape[1]
    window_start = lax.axis_index(("col", "sub")) * leaves_here - leaves_here
    widened = with_halo(vectors, ((("col", "sub"), 0),), leaves_here * leaf_rows)
    window_vec = widened.reshape(3 * leaves_here, leaf_rows, columns)
    own_vec = vectors.reshape(leaves_here, leaf_rows, columns)
    leaf_coefs = jnp.einsum("lrp,lpc->lrc", leaf_basis, own_vec, preferred_element_type=jnp.float32)
    window_coefs = with_halo(leaf_coefs, ((("col", "sub"), 0),), leaves_here)
    cluster_coef = jnp.einsum("lrs,lrc->sc", leaf_transfer, leaf_coefs, precision=HIGHEST)
    sub_coefs = lax.all_gather(cluster_coef[None], "sub", axis=0, tiled=True)
    cluster_field = jnp.einsum(
        "krs,ksc->rc", cluster_coupling[0], sub_coefs[cluster_partner[0]], precision=HIGHEST
    )
    upward = jnp.dot(cluster_transfer[0].T, cluster_coef, precision=HIGHEST)
    top_coef = lax.psum(upward, "sub")
    col_coefs = lax.all_gather(top_coef[None], "col", axis=0, tiled=True)
    top_field = jnp.einsum(
        "krs,ksc->rc", top_coupling[0], col_coefs[top_partner[0]], precision=HIGHEST
    )
    cluster_field = cluster_field + jnp.dot(cluster_transfer[0], top_field, precision=HIGHEST)
    far_coefs = window_coefs[leaf_far - window_start]
    leaf_field = jnp.einsum("lkrs,lksc->lrc", leaf_coupling, far_coefs, precision=HIGHEST)
    leaf_field = leaf_field + jnp.einsum(
        "lrs,sc->lrc", leaf_transfer, cluster_field, precision=HIGHEST
    )
    rounded = leaf_field.astype(jnp.bfloat16)
    picked = window_vec[near_index - window_start]
    near_part = jnp.einsum(
        "lkij,lkjc->lic", near_blocks, picked, preferred_element_type=jnp.float32
    )
    far_part = jnp.einsum("lrp,lrc->lpc", leaf_basis, rounded, preferred_element_type=jnp.float32)
    return (near_part + far_part).astype(jnp.bfloat16).reshape(leaves_here * leaf_rows, columns)


def solution(mesh):
    in_specs = (
        P(("col", "sub"), None),
        P(("col", "sub"), None, None, None),
        P(("col", "sub"), None),
        P(("col", "sub"), None, None),
        P(("col", "sub"), None, None),
        P(("col", "sub"), None, None, None),
        P(("col", "sub"), None),
        P(("col", "sub"), None, None),
        P(("col", "sub"), None, None, None),
        P(("col", "sub"), None),
        P("col", None, None, None),
        P("col", None),
    )
    out_specs = P(("col", "sub"), None)
    return jax.shard_map(local, mesh=mesh, in_specs=in_specs, out_specs=out_specs, check_vma=False)
```

profile of v0, /device:TPU:1, one launch (start us, length us, event | category | flops | bytes accessed | tf_op | source)
XLA Modules:
  0.0 154.2 jit_solution(7868082268854348627)
XLA Ops:
  0.0 0.0 copy-start
  0.0 0.0 copy-start.5
  0.0 0.0 copy-start.4
  0.0 1.7 %fusion.12 = f32[16,32,128]{2,1,0:T(8,128)S(1)} fusion(bf16[16,32,256]{2,1,0:T(8,128)(2,1)} %param.15, bf16[16,256,128]{2,1,0:T(8,128)(2,1)} %bitcast.79), kind=kOutput, calls=%fused_computation.33 | convolution fusion | flops 33554432 | bytes 1572864 | tf_op jit(solution)/shard_map/lrp,lpc->lrc/dot_general | solution.py:43
  1.7 8.9 %collective-permute-start.3 = (f32[16,32,128]{2,1,0:T(8,128)S(1)}, f32[16,32,128]{2,1,0:T(8,128)S(1)}, u32[]{:S(2)}, u32[]{:S(2)}) collective-permute-start(f32[16,32,128]{2,1,0:T(8,128)S(1)} %fusion.12), channel_id=1, source_target_pairs={{1,0},{2,1},{3,2},{4,3},{5,4},{6,5},{7,6},{8,7},{9,8},{10,9},{11,1... | collective-permute-start | bytes 786440 | tf_op jit(solution)/shard_map/ppermute | solution.py:17
  10.6 1.9 %collective-permute-start.2 = (f32[16,32,128]{2,1,0:T(8,128)S(1)}, f32[16,32,128]{2,1,0:T(8,128)}, u32[]{:S(2)}, u32[]{:S(2)}) collective-permute-start(f32[16,32,128]{2,1,0:T(8,128)S(1)} %fusion.12), channel_id=1, source_target_pairs={{0,1},{1,2},{2,3},{3,4},{4,5},{5,6},{6,7},{7,8},{8,9},{9,10},{10,1... | collective-permute-start | bytes 786440 | tf_op jit(solution)/shard_map/ppermute | solution.py:14
  12.5 4.9 %collective-permute-start.1 = (bf16[4096,128]{1,0:T(8,128)(2,1)}, bf16[4096,128]{1,0:T(8,128)(2,1)}, u32[]{:S(2)}, u32[]{:S(2)}) collective-permute-start(bf16[4096,128]{1,0:T(8,128)(2,1)} %param.12), channel_id=1, source_target_pairs={{1,0},{2,1},{3,2},{4,3},{5,4},{6,5},{7,6},{8,7},{9,8},{10,9},{11,1... | collective-permute-start | bytes 3145736 | tf_op jit(solution)/shard_map/ppermute | solution.py:17
  17.4 1.9 %collective-permute-start = (bf16[4096,128]{1,0:T(8,128)(2,1)}, bf16[4096,128]{1,0:T(8,128)(2,1)}, u32[]{:S(2)}, u32[]{:S(2)}) collective-permute-start(bf16[4096,128]{1,0:T(8,128)(2,1)} %param.12), channel_id=1, source_target_pairs={{0,1},{1,2},{2,3},{3,4},{4,5},{5,6},{6,7},{7,8},{8,9},{9,10},{10,1... | collective-permute-start | bytes 3145736 | tf_op jit(solution)/shard_map/ppermute | solution.py:14
  19.3 0.7 fusion.10
  20.0 0.7 fusion.11
  20.7 1.3 compare_select_fusion.1
  21.9 0.7 compare_select_fusion
  22.6 0.6 pad_clamp_fusion
  23.2 0.1 copy.24
  23.3 0.6 reshape.78
  23.9 1.5 fusion.13
  25.4 0.9 convolution_bitcast_fusion.3
  26.4 35.0 %psum.7 = f32[1,32,128]{2,1,0:T(8,128)S(1)} all-reduce(f32[1,32,128]{2,1,0:T(8,128)S(1)} %convolution_bitcast_fusion.3), channel_id=1, replica_groups=mesh['col'=32,'sub'=8] {'sub'}, use_global_device_ids=true, to_apply=%region_0.0 | all-reduce | flops 4096 | bytes 32768 | tf_op jit(solution)/shard_map/psum | solution.py:51
  61.4 18.5 %all-gather = f32[256,128]{1,0:T(8,128)S(1)} all-gather(f32[32,128]{1,0:T(8,128)S(1)} %bitcast.81), channel_id=2, replica_groups=mesh['col'=32,'sub'=8] {'sub'}, dimensions={0}, use_global_device_ids=true | all-gather | bytes 147456 | tf_op jit(solution)/shard_map/all_gather | solution.py:46
  79.9 36.2 %all_gather.7 = f32[32,32,128]{2,1,0:T(8,128)S(1)} all-gather(f32[1,32,128]{2,1,0:T(8,128)S(1)} %psum.7), channel_id=1, replica_groups=mesh['col'=32,'sub'=8] {'col'}, dimensions={0}, use_global_device_ids=true | all-gather | bytes 540672 | tf_op jit(solution)/shard_map/all_gather | solution.py:52
  116.1 0.6 gather_fusion.2
  116.6 0.0 copy-done.5
  116.6 0.2 convolution_bitcast_fusion.4
  116.9 0.7 gather_fusion.3
  117.6 0.0 copy-done.4
  117.6 0.3 convolution_bitcast_fusion.2
  117.9 0.6 pad_clamp_fusion.2
  118.5 0.7 copy.22
  119.3 0.1 reshape.70
  119.4 0.9 fusion.4
  120.2 0.0 collective-permute-done.3
  120.3 0.0 collective-permute-done.2
  120.3 1.0 pad_maximum_fusion.1
  121.3 2.1 %gather_fusion.1 = f32[128,32,128]{2,1,0:T(8,128)} fusion(f32[48,32,128]{2,1,0:T(8,128)S(1)} %pad_maximum_fusion.1, s32[1024]{0:T(1024)S(1)} %pad_clamp_fusion.2), kind=kCustom, calls=%fused_computation.1 | custom fusion | bytes 4194816 | tf_op jit(solution)/shard_map/gather | solution.py:57
  123.4 0.0 copy-start.3
  123.4 0.0 copy-start.2
  123.4 0.0 copy-done
  123.4 0.0 copy-start.1
  123.4 4.4 %convolution_bitcast_fusion.1 = f32[16,32,128]{2,1,0:T(8,128)S(1)} fusion(f32[16,8,32,128]{3,2,1,0:T(8,128)} %bitcast.78, f32[16,8,32,32]{3,2,1,0:T(8,128)S(1)} %copy-done), kind=kOutput, calls=%fused_computation.10 | convolution fusion | flops 201326592 | bytes 2883584 | tf_op jit(solution)/shard_map/lkrs,lksc->lrc/dot_general | solution.py:58
  127.9 0.0 copy-done.3
  127.9 0.4 fusion.3
  128.2 0.0 copy-done.2
  128.2 1.9 %fusion.14 = f32[16,128,256]{2,1,0:T(8,128)} fusion(bf16[16,32,128]{2,1,0:T(8,128)(2,1)S(1)} %fusion.3, bf16[16,32,256]{2,1,0:T(8,128)(2,1)S(1)} %copy-done.2), kind=kOutput, calls=%fused_computation.35 | convolution fusion | flops 33554432 | bytes 2490368 | tf_op jit(solution)/shard_map/lrp,lrc->lpc/dot_general | solution.py:67
  130.1 0.0 collective-permute-done.1
  130.1 0.0 collective-permute-done
  130.1 0.0 copy-done.1
  130.1 9.8 %pad_maximum_fusion = bf16[12288,128]{1,0:T(8,128)(2,1)} fusion(bf16[4096,128]{1,0:T(8,128)(2,1)} %collective-permute-done.1, bf16[4096,128]{1,0:T(8,128)(2,1)S(1)} %copy-done.1, bf16[4096,128]{1,0:T(8,128)(2,1)} %collective-permute-done), kind=kLoop, calls=%fused_computation.4 | loop fusion | flops 9437184 | bytes 6291456 | tf_op jit(solution)/shard_map/concatenate | solution.py:18
  139.9 4.9 %gather_fusion = bf16[64,256,128]{2,1,0:T(8,128)(2,1)} fusion(bf16[48,256,128]{2,1,0:T(8,128)(2,1)} %bitcast.76, s32[1024]{0:T(1024)S(1)} %pad_clamp_fusion.3), kind=kCustom, calls=%fused_computation | custom fusion | bytes 8388864 | tf_op jit(solution)/shard_map/gather | solution.py:63
  144.8 8.1 %fusion.1 = bf16[16,256,128]{1,2,0:T(8,128)(2,1)S(1)} fusion(f32[16,128,256]{2,1,0:T(8,128)} %fusion.14, bf16[16,4,256,128]{3,2,1,0:T(8,128)(2,1)} %bitcast.77, bf16[16,4,256,256]{3,2,1,0:T(8,128)(2,1)} %param.13), kind=kOutput, calls=%fused_computation.7 | convolution fusion | flops 1074790400 | bytes 15728640 | tf_op jit(solution)/shard_map/lkij,lkjc->lic/dot_general | solution.py:64
  152.9 1.3 copy.26
  (2 shorter events, 0.0 us)
Async XLA Ops:
  0.0 123.4 %copy-start = (f32[16,8,32,32]{3,2,1,0:T(8,128)S(1)}, f32[16,8,32,32]{3,2,1,0:T(8,128)}, u32[]{:S(2)}) copy-start(f32[16,8,32,32]{3,2,1,0:T(8,128)} %param.17) | copy-start | bytes 1572868
  0.0 116.6 %copy-start.5 = (f32[1,4,32,32]{3,2,1,0:T(8,128)S(1)}, f32[1,4,32,32]{3,2,1,0:T(8,128)}, u32[]{:S(2)}) copy-start(f32[1,4,32,32]{3,2,1,0:T(8,128)} %param.20) | copy-start | bytes 49156
  0.0 117.6 %copy-start.4 = (f32[1,8,32,32]{3,2,1,0:T(8,128)S(1)}, f32[1,8,32,32]{3,2,1,0:T(8,128)}, u32[]{:S(2)}) copy-start(f32[1,8,32,32]{3,2,1,0:T(8,128)} %param.22) | copy-start | bytes 98308
  1.7 118.5 %collective-permute-start.3 = (f32[16,32,128]{2,1,0:T(8,128)S(1)}, f32[16,32,128]{2,1,0:T(8,128)S(1)}, u32[]{:S(2)}, u32[]{:S(2)}) collective-permute-start(f32[16,32,128]{2,1,0:T(8,128)S(1)} %fusion.12), channel_id=1, source_target_pairs={{1,0},{2,1},{3,2},{4,3},{5,4},{6,5},{7,6},{8,7},{9,8},{10,9},{11,1... | collective-permute-start | bytes 786440 | tf_op jit(solution)/shard_map/ppermute | solution.py:17
  10.6 109.6 %collective-permute-start.2 = (f32[16,32,128]{2,1,0:T(8,128)S(1)}, f32[16,32,128]{2,1,0:T(8,128)}, u32[]{:S(2)}, u32[]{:S(2)}) collective-permute-start(f32[16,32,128]{2,1,0:T(8,128)S(1)} %fusion.12), channel_id=1, source_target_pairs={{0,1},{1,2},{2,3},{3,4},{4,5},{5,6},{6,7},{7,8},{8,9},{9,10},{10,1... | collective-permute-start | bytes 786440 | tf_op jit(solution)/shard_map/ppermute | solution.py:14
  12.5 117.6 %collective-permute-start.1 = (bf16[4096,128]{1,0:T(8,128)(2,1)}, bf16[4096,128]{1,0:T(8,128)(2,1)}, u32[]{:S(2)}, u32[]{:S(2)}) collective-permute-start(bf16[4096,128]{1,0:T(8,128)(2,1)} %param.12), channel_id=1, source_target_pairs={{1,0},{2,1},{3,2},{4,3},{5,4},{6,5},{7,6},{8,7},{9,8},{10,9},{11,1... | collective-permute-start | bytes 3145736 | tf_op jit(solution)/shard_map/ppermute | solution.py:17
  17.4 112.7 %collective-permute-start = (bf16[4096,128]{1,0:T(8,128)(2,1)}, bf16[4096,128]{1,0:T(8,128)(2,1)}, u32[]{:S(2)}, u32[]{:S(2)}) collective-permute-start(bf16[4096,128]{1,0:T(8,128)(2,1)} %param.12), channel_id=1, source_target_pairs={{0,1},{1,2},{2,3},{3,4},{4,5},{5,6},{6,7},{7,8},{8,9},{9,10},{10,1... | collective-permute-start | bytes 3145736 | tf_op jit(solution)/shard_map/ppermute | solution.py:14
  123.4 4.4 %copy-start.3 = (f32[16,32,32]{2,1,0:T(8,128)S(1)}, f32[16,32,32]{2,1,0:T(8,128)}, u32[]{:S(2)}) copy-start(f32[16,32,32]{2,1,0:T(8,128)} %param.16) | copy-start | bytes 196612
  123.4 4.8 %copy-start.2 = (bf16[16,32,256]{2,1,0:T(8,128)(2,1)S(1)}, bf16[16,32,256]{2,1,0:T(8,128)(2,1)}, u32[]{:S(2)}) copy-start(bf16[16,32,256]{2,1,0:T(8,128)(2,1)} %param.15) | copy-start | bytes 786436
  123.4 6.7 %copy-start.1 = (bf16[4096,128]{1,0:T(8,128)(2,1)S(1)}, bf16[4096,128]{1,0:T(8,128)(2,1)}, u32[]{:S(2)}) copy-start(bf16[4096,128]{1,0:T(8,128)(2,1)} %param.12) | copy-start | bytes 3145732
where the time goes:
time: 155 us; the launch traced here: 154 us
  blocking collectives  89.7 us (58%)
  matrix products  20.3 us (13%)
  starting transfers between devices  17.6 us (11%)
  other arithmetic  15.3 us (10%)
  local copies, waits for them, and re-layouts  11.1 us (7%)
    all_gather x1, blocking collectives, local(): col_coefs = lax.all_gather(top_coef[None], 'col', axis=0, tiled=True)  36.2 us
    psum x1, blocking collectives, local(): top_coef = lax.psum(upward, 'sub')  35 us
    all_gather x1, blocking collectives, local(): sub_coefs = lax.all_gather(cluster_coef[None], 'sub', axis=0, tiled=True)  18.5 us
    ppermute x2, starting transfers between devices, with_halo(): lax.ppermute(lax.slice_in_dim(block, 0, width, axis=dim), axis, backward)  13.7 us
    concatenate x2, other arithmetic, with_halo(): block = jnp.concatenate([low, block, high], axis=dim)  10.8 us
    dot_general x1, matrix products, local(): jnp.einsum('lkij,lkjc->lic', near_blocks, picked, preferred_element_type=...  8.06 us
    gather x1, local copies, waits for them, and re-layouts, local(): picked = window_vec[near_index - window_start]  4.91 us
    dot_general x1, matrix products, local(): jnp.einsum('lkrs,lksc->lrc', leaf_coupling, far_coefs, precision=HIGHEST)  4.43 us
  transfers between devices with their start and end apart: 4, of which 0 were waited for; matrix products, arithmetic and copies ran while one was open for 14% of the time, Pallas kernels for 0%

commit v1 on v0

--- a/solution.py
+++ b/solution.py
@@ -1,9 +1,25 @@
+import functools
 import jax
 import jax.numpy as jnp
 from jax import lax
 from jax.sharding import PartitionSpec as P
 
 HIGHEST = lax.Precision.HIGHEST
+
+
+def advance_ports_up(local_values, row_axis):
+    return jnp.concatenate(
+        jax.lax.all_to_all(
+            jnp.stack([local_values for _ in range(jax.lax.psum(1, axis_name=row_axis))]),
+            axis_name=row_axis,
+            split_axis=0,
+            concat_axis=0,
+        ),
+        0,
+    )
+
+
+pack_object_all = functools.partial(advance_ports_up, row_axis="sub")
 
 
 def with_halo(block, sides, width):
@@ -43,7 +59,7 @@
     leaf_coefs = jnp.einsum("lrp,lpc->lrc", leaf_basis, own_vec, preferred_element_type=jnp.float32)
     window_coefs = with_halo(leaf_coefs, ((("col", "sub"), 0),), leaves_here)
     cluster_coef = jnp.einsum("lrs,lrc->sc", leaf_transfer, leaf_coefs, precision=HIGHEST)
-    sub_coefs = lax.all_gather(cluster_coef[None], "sub", axis=0, tiled=True)
+    sub_coefs = pack_object_all(cluster_coef[None])
     cluster_field = jnp.einsum(
         "krs,ksc->rc", cluster_coupling[0], sub_coefs[cluster_partner[0]], precision=HIGHEST
     )

time: 155 us -> 132 us (0.85)
  blocking collectives: 89.7 us -> 63.3 us
  starting transfers between devices: 17.6 us -> 23 us
  other arithmetic: 15.3 us -> 13.5 us
    all_gather x1 -> x0, blocking collectives: 18.5 us -> none  [local(): sub_coefs = lax.all_gather(cluster_coef[None], 'sub', axis=0, tiled=True)]
    all_gather x1, blocking collectives: 36.2 us -> 30.1 us  [local(): col_coefs = lax.all_gather(top_coef[None], 'col', axis=0, tiled=True)]
    all_to_all x0 -> x1, starting transfers between devices: none -> 5.46 us  [advance_ports_up(): jax.lax.all_to_all(jnp.stack([local_values for _ in range(jax.lax.psum(1,...]
    psum x1, blocking collectives: 35 us -> 33.2 us  [local(): top_coef = lax.psum(upward, 'sub')]
  transfers between devices with their start and end apart: 4 -> 5, of which waited for: 0 -> 0; matrix products, arithmetic and copies ran while one was open for 14% -> 15% of each run, Pallas kernels for 0% -> 0%
where the time goes in v1:
time: 132 us
  blocking collectives  63.3 us (48%)
  starting transfers between devices  23 us (17%)
  matrix products  21.2 us (16%)
  other arithmetic  13.5 us (10%)
  local copies, waits for them, and re-layouts  10.5 us (8%)
    psum x1, blocking collectives, local(): top_coef = lax.psum(upward, 'sub')  33.2 us
    all_gather x1, blocking collectives, local(): col_coefs = lax.all_gather(top_coef[None], 'col', axis=0, tiled=True)  30.1 us
    ppermute x2, starting transfers between devices, with_halo(): lax.ppermute(lax.slice_in_dim(block, 0, width, axis=dim), axis, backward)  13.7 us
    concatenate x2, other arithmetic, with_halo(): block = jnp.concatenate([low, block, high], axis=dim)  10.8 us
    dot_general x1, matrix products, local(): jnp.einsum('lkij,lkjc->lic', near_blocks, picked, preferred_element_type=...  8.07 us
    all_to_all x1, starting transfers between devices, advance_ports_up(): jax.lax.all_to_all(jnp.stack([local_values for _ in range(jax.lax.psum(1,...  5.46 us
    gather x1, local copies, waits for them, and re-layouts, local(): picked = window_vec[near_index - window_start]  4.91 us
    dot_general x1, matrix products, local(): jnp.einsum('lkrs,lksc->lrc', leaf_coupling, far_coefs, precision=HIGHEST)  4.43 us
  transfers between devices with their start and end apart: 5, of which 0 were waited for; matrix products, arithmetic and copies ran while one was open for 15% of the time, Pallas kernels for 0%

profile of v1, /device:TPU:1, one launch (start us, length us, event | category | flops | bytes accessed | tf_op | source)
XLA Modules:
  0.0 131.6 jit_solution(12802998101694507040)
XLA Ops:
  0.0 0.0 copy-start
  0.0 0.0 copy-start.4
  0.0 1.7 %fusion.12 = f32[16,32,128]{2,1,0:T(8,128)S(1)} fusion(bf16[16,32,256]{2,1,0:T(8,128)(2,1)} %param.15, bf16[16,256,128]{2,1,0:T(8,128)(2,1)} %bitcast.79), kind=kOutput, calls=%fused_computation.33 | convolution fusion | flops 33554432 | bytes 1572864 | tf_op jit(solution)/shard_map/lrp,lpc->lrc/dot_general | solution.py:59
  1.7 8.9 %collective-permute-start.3 = (f32[16,32,128]{2,1,0:T(8,128)S(1)}, f32[16,32,128]{2,1,0:T(8,128)S(1)}, u32[]{:S(2)}, u32[]{:S(2)}) collective-permute-start(f32[16,32,128]{2,1,0:T(8,128)S(1)} %fusion.12), channel_id=1, source_target_pairs={{1,0},{2,1},{3,2},{4,3},{5,4},{6,5},{7,6},{8,7},{9,8},{10,9},{11,1... | collective-permute-start | bytes 786440 | tf_op jit(solution)/shard_map/ppermute | solution.py:33
  10.6 1.9 %collective-permute-start.2 = (f32[16,32,128]{2,1,0:T(8,128)S(1)}, f32[16,32,128]{2,1,0:T(8,128)}, u32[]{:S(2)}, u32[]{:S(2)}) collective-permute-start(f32[16,32,128]{2,1,0:T(8,128)S(1)} %fusion.12), channel_id=1, source_target_pairs={{0,1},{1,2},{2,3},{3,4},{4,5},{5,6},{6,7},{7,8},{8,9},{9,10},{10,1... | collective-permute-start | bytes 786440 | tf_op jit(solution)/shard_map/ppermute | solution.py:30
  12.5 4.9 %collective-permute-start.1 = (bf16[4096,128]{1,0:T(8,128)(2,1)}, bf16[4096,128]{1,0:T(8,128)(2,1)}, u32[]{:S(2)}, u32[]{:S(2)}) collective-permute-start(bf16[4096,128]{1,0:T(8,128)(2,1)} %param.12), channel_id=1, source_target_pairs={{1,0},{2,1},{3,2},{4,3},{5,4},{6,5},{7,6},{8,7},{9,8},{10,9},{11,1... | collective-permute-start | bytes 3145736 | tf_op jit(solution)/shard_map/ppermute | solution.py:33
  17.4 1.9 %collective-permute-start = (bf16[4096,128]{1,0:T(8,128)(2,1)}, bf16[4096,128]{1,0:T(8,128)(2,1)}, u32[]{:S(2)}, u32[]{:S(2)}) collective-permute-start(bf16[4096,128]{1,0:T(8,128)(2,1)} %param.12), channel_id=1, source_target_pairs={{0,1},{1,2},{2,3},{3,4},{4,5},{5,6},{6,7},{7,8},{8,9},{9,10},{10,1... | collective-permute-start | bytes 3145736 | tf_op jit(solution)/shard_map/ppermute | solution.py:30
  19.3 1.5 %fusion.13 = f32[128,32,1]{0,1,2:T(8,128)S(1)} fusion(f32[16,32,128]{2,1,0:T(8,128)S(1)} %fusion.12, f32[16,32,32]{2,1,0:T(8,128)} %param.16), kind=kOutput, calls=%fused_computation.34 | convolution fusion | flops 25165824 | bytes 344064 | tf_op jit(solution)/shard_map/lrs,lrc->sc/dot_general | solution.py:61
  20.9 0.7 stack.3
  21.5 5.5 %all-to-all-start = ((f32[8,1,32,128]{3,2,1,0:T(8,128)}), f32[8,1,32,128]{3,2,1,0:T(8,128)S(1)}, u32[]{:S(2)}, u32[]{:S(2)}) async-start(f32[8,1,32,128]{3,2,1,0:T(8,128)} %stack.3), calls=%async_computation | async-start | bytes 262144 | tf_op jit(solution)/shard_map/all_to_all | solution.py:12
  27.0 0.7 fusion.10
  27.6 0.7 fusion.11
  28.3 0.7 compare_select_fusion.1
  29.0 0.7 compare_select_fusion
  29.7 0.1 copy.24
  29.8 0.1 reshape.84
  29.9 0.1 copy.22
  30.0 0.1 reshape.76
  30.0 0.9 convolution_bitcast_fusion.3
  31.0 33.2 %psum.7 = f32[1,32,128]{2,1,0:T(8,128)S(1)} all-reduce(f32[1,32,128]{2,1,0:T(8,128)S(1)} %convolution_bitcast_fusion.3), channel_id=1, replica_groups=mesh['col'=32,'sub'=8] {'sub'}, use_global_device_ids=true, to_apply=%region_0.0 | all-reduce | flops 4096 | bytes 32768 | tf_op jit(solution)/shard_map/psum | solution.py:67
  64.2 30.1 %all_gather.3 = f32[32,32,128]{2,1,0:T(8,128)S(1)} all-gather(f32[1,32,128]{2,1,0:T(8,128)S(1)} %psum.7), channel_id=1, replica_groups=mesh['col'=32,'sub'=8] {'col'}, dimensions={0}, use_global_device_ids=true | all-gather | bytes 540672 | tf_op jit(solution)/shard_map/all_gather | solution.py:68
  94.2 0.6 gather_fusion.3
  94.8 0.0 copy-done.4
  94.8 0.3 convolution_bitcast_fusion.2
  95.2 0.0 all-to-all-done
  95.2 0.6 gather_fusion.2
  95.7 1.1 convolution_bitcast_fusion.4
  96.8 0.9 fusion.4
  97.7 0.0 collective-permute-done.3
  97.7 0.0 collective-permute-done.2
  97.7 1.0 pad_maximum_fusion.1
  98.7 2.1 %gather_fusion.1 = f32[128,32,128]{2,1,0:T(8,128)} fusion(f32[48,32,128]{2,1,0:T(8,128)S(1)} %pad_maximum_fusion.1, s32[1024]{0:T(1024)S(1)} %pad_clamp_fusion.2), kind=kCustom, calls=%fused_computation.1 | custom fusion | bytes 4194816 | tf_op jit(solution)/shard_map/gather | solution.py:73
  100.9 0.0 copy-start.3
  100.9 0.0 copy-start.2
  100.9 0.0 copy-done
  100.9 0.0 copy-start.1
  100.9 4.4 %convolution_bitcast_fusion.1 = f32[16,32,128]{2,1,0:T(8,128)S(1)} fusion(f32[16,8,32,128]{3,2,1,0:T(8,128)} %bitcast.78, f32[16,8,32,32]{3,2,1,0:T(8,128)S(1)} %copy-done), kind=kOutput, calls=%fused_computation.10 | convolution fusion | flops 201326592 | bytes 2883584 | tf_op jit(solution)/shard_map/lkrs,lksc->lrc/dot_general | solution.py:74
  105.3 0.0 copy-done.3
  105.3 0.4 fusion.3
  105.7 0.0 copy-done.2
  105.7 1.9 %fusion.14 = f32[16,128,256]{2,1,0:T(8,128)} fusion(bf16[16,32,128]{2,1,0:T(8,128)(2,1)S(1)} %fusion.3, bf16[16,32,256]{2,1,0:T(8,128)(2,1)S(1)} %copy-done.2), kind=kOutput, calls=%fused_computation.35 | convolution fusion | flops 33554432 | bytes 2490368 | tf_op jit(solution)/shard_map/lrp,lrc->lpc/dot_general | solution.py:83
  107.6 0.0 collective-permute-done.1
  107.6 0.0 collective-permute-done
  107.6 0.0 copy-done.1
  107.6 9.8 %pad_maximum_fusion = bf16[12288,128]{1,0:T(8,128)(2,1)} fusion(bf16[4096,128]{1,0:T(8,128)(2,1)} %collective-permute-done.1, bf16[4096,128]{1,0:T(8,128)(2,1)S(1)} %copy-done.1, bf16[4096,128]{1,0:T(8,128)(2,1)} %collective-permute-done), kind=kLoop, calls=%fused_computation.4 | loop fusion | flops 9437184 | bytes 6291456 | tf_op jit(solution)/shard_map/concatenate | solution.py:34
  117.4 4.9 %gather_fusion = bf16[64,256,128]{2,1,0:T(8,128)(2,1)} fusion(bf16[48,256,128]{2,1,0:T(8,128)(2,1)} %bitcast.76, s32[1024]{0:T(1024)S(1)} %pad_clamp_fusion.3), kind=kCustom, calls=%fused_computation | custom fusion | bytes 8388864 | tf_op jit(solution)/shard_map/gather | solution.py:79
  122.3 8.1 %fusion.1 = bf16[16,256,128]{1,2,0:T(8,128)(2,1)S(1)} fusion(f32[16,128,256]{2,1,0:T(8,128)} %fusion.14, bf16[16,4,256,128]{3,2,1,0:T(8,128)(2,1)} %bitcast.77, bf16[16,4,256,256]{3,2,1,0:T(8,128)(2,1)} %param.13), kind=kOutput, calls=%fused_computation.7 | convolution fusion | flops 1074790400 | bytes 15728640 | tf_op jit(solution)/shard_map/lkij,lkjc->lic/dot_general | solution.py:80
  130.3 1.3 copy.26
  (4 shorter events, 0.0 us)
Async XLA Ops:
  0.0 100.9 %copy-start = (f32[16,8,32,32]{3,2,1,0:T(8,128)S(1)}, f32[16,8,32,32]{3,2,1,0:T(8,128)}, u32[]{:S(2)}) copy-start(f32[16,8,32,32]{3,2,1,0:T(8,128)} %param.17) | copy-start | bytes 1572868
  0.0 94.8 %copy-start.4 = (f32[1,8,32,32]{3,2,1,0:T(8,128)S(1)}, f32[1,8,32,32]{3,2,1,0:T(8,128)}, u32[]{:S(2)}) copy-start(f32[1,8,32,32]{3,2,1,0:T(8,128)} %param.22) | copy-start | bytes 98308
  1.7 96.0 %collective-permute-start.3 = (f32[16,32,128]{2,1,0:T(8,128)S(1)}, f32[16,32,128]{2,1,0:T(8,128)S(1)}, u32[]{:S(2)}, u32[]{:S(2)}) collective-permute-start(f32[16,32,128]{2,1,0:T(8,128)S(1)} %fusion.12), channel_id=1, source_target_pairs={{1,0},{2,1},{3,2},{4,3},{5,4},{6,5},{7,6},{8,7},{9,8},{10,9},{11,1... | collective-permute-start | bytes 786440 | tf_op jit(solution)/shard_map/ppermute | solution.py:33
  10.6 87.1 %collective-permute-start.2 = (f32[16,32,128]{2,1,0:T(8,128)S(1)}, f32[16,32,128]{2,1,0:T(8,128)}, u32[]{:S(2)}, u32[]{:S(2)}) collective-permute-start(f32[16,32,128]{2,1,0:T(8,128)S(1)} %fusion.12), channel_id=1, source_target_pairs={{0,1},{1,2},{2,3},{3,4},{4,5},{5,6},{6,7},{7,8},{8,9},{9,10},{10,1... | collective-permute-start | bytes 786440 | tf_op jit(solution)/shard_map/ppermute | solution.py:30
  12.5 95.0 %collective-permute-start.1 = (bf16[4096,128]{1,0:T(8,128)(2,1)}, bf16[4096,128]{1,0:T(8,128)(2,1)}, u32[]{:S(2)}, u32[]{:S(2)}) collective-permute-start(bf16[4096,128]{1,0:T(8,128)(2,1)} %param.12), channel_id=1, source_target_pairs={{1,0},{2,1},{3,2},{4,3},{5,4},{6,5},{7,6},{8,7},{9,8},{10,9},{11,1... | collective-permute-start | bytes 3145736 | tf_op jit(solution)/shard_map/ppermute | solution.py:33
  17.4 90.2 %collective-permute-start = (bf16[4096,128]{1,0:T(8,128)(2,1)}, bf16[4096,128]{1,0:T(8,128)(2,1)}, u32[]{:S(2)}, u32[]{:S(2)}) collective-permute-start(bf16[4096,128]{1,0:T(8,128)(2,1)} %param.12), channel_id=1, source_target_pairs={{0,1},{1,2},{2,3},{3,4},{4,5},{5,6},{6,7},{7,8},{8,9},{9,10},{10,1... | collective-permute-start | bytes 3145736 | tf_op jit(solution)/shard_map/ppermute | solution.py:30
  21.5 73.6 %all-to-all-start = ((f32[8,1,32,128]{3,2,1,0:T(8,128)}), f32[8,1,32,128]{3,2,1,0:T(8,128)S(1)}, u32[]{:S(2)}, u32[]{:S(2)}) async-start(f32[8,1,32,128]{3,2,1,0:T(8,128)} %stack.3), calls=%async_computation | async-start | bytes 262144 | tf_op jit(solution)/shard_map/all_to_all | solution.py:12
  100.9 4.4 %copy-start.3 = (f32[16,32,32]{2,1,0:T(8,128)S(1)}, f32[16,32,32]{2,1,0:T(8,128)}, u32[]{:S(2)}) copy-start(f32[16,32,32]{2,1,0:T(8,128)} %param.16) | copy-start | bytes 196612
  100.9 4.8 %copy-start.2 = (bf16[16,32,256]{2,1,0:T(8,128)(2,1)S(1)}, bf16[16,32,256]{2,1,0:T(8,128)(2,1)}, u32[]{:S(2)}) copy-start(bf16[16,32,256]{2,1,0:T(8,128)(2,1)} %param.15) | copy-start | bytes 786436
  100.9 6.7 %copy-start.1 = (bf16[4096,128]{1,0:T(8,128)(2,1)S(1)}, bf16[4096,128]{1,0:T(8,128)(2,1)}, u32[]{:S(2)}) copy-start(bf16[4096,128]{1,0:T(8,128)(2,1)} %param.12) | copy-start | bytes 3145732
